TPU v7x, 128 devices: a whole 4x4x4 slice. The times are simulated.
128 devices in a mesh: llm: 4 (over x), enc: 32 (over y, z, core).
Axes of the slice: x: 4, y: 4, z: 4, core: 2. Of those that a mesh axis runs over, the one named last changes fastest.
Arguments:
- token_gradient: bfloat16 [256, 128, 8192], P('enc', None, 'llm'), may hold values from -6 to 6
- projection: bfloat16 [1280, 8192], P(None, 'llm'), may hold values from -0.0625 to 0.0625
- clip_length: int32 [512], P('enc'), may hold values from 16 to 32, as said below
- clip_offset: int32 [512], P('enc'), may hold values from 0 to 96, as said below
- clip_home: int32 [512], P('enc'), may hold values from 0 to 511, as said below
- block_input: bfloat16 [512, 32, 1280], P('enc'), may hold values from -6 to 6
- block_output: bfloat16 [512, 32, 1280], P('enc'), may hold values from -6 to 6
- norm_gain: float32 [1280], replicated, may hold values from 0.1 to 1.9
- norm_bias: float32 [1280], replicated, may hold values from -3 to 3
- up_weight: bfloat16 [1280, 5120], P('enc', 'llm'), may hold values from -0.15625 to 0.15625
- up_bias: float32 [5120], P('llm'), may hold values from -3 to 3
- down_weight: bfloat16 [5120, 1280], P('llm', 'enc'), may hold values from -0.078125 to 0.078125
- post_gain: float32 [1280], replicated, may hold values from 0.1 to 1.9
Outputs:
- input_gradient: bfloat16 [512, 32, 1280], P('enc', None, 'llm')
- up_gradient: float32 [1280, 5120], P('enc', 'llm')
- down_gradient: float32 [5120, 1280], P('llm', 'enc')
Inputs may be any that keep to these rules, and one draw needn't show every extreme that they name: `clip_length`: each entry of an aligned block of 16 entries is at most 32, and every block holds one entry equal to 32. Clip k starts in part k % 2 of its sequence, the parts being 64 rows long, and clip_offset + 32 stays within that part. `clip_home`: A permutation of the 512 encoder slots; slot j belongs to encoder index j // 16; the clips of one aligned block of 16 entries go to one encoder index at most 1 times, and some encoder index receives exactly 1 of them.
All inputs are finite; a program needn't handle non-finite values.
Results may differ from a plain program's by a relative error of at most 0.0068.
Values may be sent and summed in bfloat16 or wider, within the bound.
No kernel may reach another device: no remote copies, remote signals or barrier semaphores. Data moves between devices by JAX's collectives and lax.ppermute only.
A program may use at most 128 MiB of HBM per device.

v0:
```python
import jax
import jax.numpy as jnp
from jax import lax
from jax.sharding import PartitionSpec as P

CPS = 2
norm_epsilon = 1e-05


def gelu_parts(pre_act):
    normal_cdf = 0.5 * (1.0 + jax.scipy.special.erf(pre_act * 0.7071067811865476))
    normal_pdf = jnp.exp(-0.5 * pre_act * pre_act) * 0.3989422804014327
    return (pre_act * normal_cdf, normal_cdf + pre_act * normal_pdf)


def norm_stats(values):
    row_mean = jnp.mean(values, axis=-1, keepdims=True)
    centred = values - row_mean
    variance = jnp.mean(centred * centred, axis=-1, keepdims=True)
    inverse = lax.rsqrt(variance + norm_epsilon)
    return (centred * inverse, inverse)


def norm_backward(grad_hat, normed_hat, inverse):
    first_mean = jnp.mean(grad_hat, axis=-1, keepdims=True)
    second_mean = jnp.mean(grad_hat * normed_hat, axis=-1, keepdims=True)
    return inverse * (grad_hat - first_mean - normed_hat * second_mean)


def row_contract(left_rows, right_rows):
    return lax.dot_general(
        left_rows, right_rows, (((0,), (0,)), ((), ())), preferred_element_type=jnp.float32
    )


def own_columns(values, column_start, column_span):
    return lax.dynamic_slice_in_dim(values, column_start, column_span, values.ndim - 1)


def project_terms(clip_blocks, projection):
    clips_here, frames, columns = clip_blocks.shape
    flat_rows = clip_blocks.reshape(clips_here * frames, columns)
    partial_terms = lax.dot_general(
        flat_rows, projection, (((1,), (1,)), ((), ())), preferred_element_type=jnp.float32
    )
    return partial_terms.reshape(clips_here, frames, projection.shape[0])


def project_sum(clip_blocks, projection):
    return lax.psum(project_terms(clip_blocks, projection), "llm")


def deliver(clip_blocks, routing, slot_marks):
    clips_here, frames, columns = clip_blocks.shape
    devices, pair_slots, slot_count = slot_marks.shape
    packed = jnp.einsum(
        "bc,cfw->bfw", routing, clip_blocks, preferred_element_type=jnp.float32
    ).astype(jnp.bfloat16)
    packed = packed.reshape(devices, pair_slots, frames, columns)
    received, marks_in = (
        lax.all_to_all(packed, "enc", split_axis=0, concat_axis=0, tiled=True),
        lax.all_to_all(slot_marks, "enc", split_axis=0, concat_axis=0, tiled=True),
    )
    placed = jnp.einsum("npc,npfw->cfw", marks_in, received, preferred_element_type=jnp.float32)
    return placed.astype(jnp.bfloat16)


def shards(
    token_gradient,
    projection,
    clip_length,
    clip_offset,
    clip_home,
    block_input,
    block_output,
    norm_gain,
    norm_bias,
    up_weight,
    up_bias,
    down_weight,
    post_gain,
):
    devices = lax.axis_size("enc")
    clips_here, frames, model_width = block_input.shape
    pair_slots = max(1, clips_here // devices)
    positions = jnp.arange(frames, dtype=jnp.int32)
    clip_order = jnp.arange(clips_here, dtype=jnp.int32)
    target = clip_home // clips_here
    slot_place = clip_home % clips_here
    earlier = clip_order[None, :] < clip_order[:, None]
    same_target = target[None, :] == target[:, None]
    bucket_rank = jnp.sum((earlier & same_target).astype(jnp.int32), axis=1)
    bucket = target * pair_slots + bucket_rank
    buckets = jnp.arange(devices * pair_slots, dtype=jnp.int32)
    routing = (buckets[:, None] == bucket[None, :]).astype(jnp.bfloat16)
    slot_table = (slot_place[:, None] == clip_order[None, :]).astype(jnp.bfloat16)
    slot_marks = jnp.dot(routing, slot_table, preferred_element_type=jnp.float32).astype(
        jnp.bfloat16
    )
    slot_marks = slot_marks.reshape(devices, pair_slots, clips_here)

    def cut_clip(clip_index, offset, length):
        picked = lax.dynamic_slice(
            token_gradient,
            (clip_index // CPS, offset, jnp.int32(0)),
            (1, frames, token_gradient.shape[2]),
        )[0]
        return jnp.where((positions < length)[:, None], picked, jnp.zeros_like(picked))

    clip_blocks = jax.vmap(cut_clip)(clip_order, clip_offset, clip_length)
    feature_grad = project_sum(deliver(clip_blocks, routing, slot_marks), projection).astype(
        jnp.bfloat16
    )
    row_total = clips_here * frames
    feature_rows = feature_grad.reshape(row_total, model_width).astype(jnp.float32)
    output_hat, output_inverse = norm_stats(
        block_output.reshape(row_total, model_width).astype(jnp.float32)
    )
    post_grad = norm_backward(feature_rows * post_gain, output_hat, output_inverse)
    post_rounded = post_grad.astype(jnp.bfloat16)
    input_hat, input_inverse = norm_stats(
        block_input.reshape(row_total, model_width).astype(jnp.float32)
    )
    normed = (input_hat * norm_gain + norm_bias).astype(jnp.bfloat16)
    up_full, down_full = (
        lax.all_gather(up_weight, "enc", axis=0, tiled=True),
        lax.all_gather(down_weight, "enc", axis=1, tiled=True),
    )
    pre_act = jnp.dot(normed, up_full, preferred_element_type=jnp.float32) + up_bias
    activation, gelu_slope = gelu_parts(pre_act)
    act_rounded = activation.astype(jnp.bfloat16)
    act_grad = lax.dot_general(
        post_rounded, down_full, (((1,), (1,)), ((), ())), preferred_element_type=jnp.float32
    )
    pre_grad = (act_grad * gelu_slope).astype(jnp.bfloat16)
    normed_part = lax.dot_general(
        pre_grad, up_full, (((1,), (1,)), ((), ())), preferred_element_type=jnp.float32
    )
    groups = lax.axis_size("llm")
    share_width = model_width // groups
    share_start = lax.axis_index("llm") * share_width
    normed_grad = lax.psum(normed_part, "llm")
    full_grad = post_grad + norm_backward(normed_grad * norm_gain, input_hat, input_inverse)
    input_rows = own_columns(full_grad, share_start, share_width)
    input_gradient = input_rows.astype(jnp.bfloat16).reshape(clips_here, frames, share_width)
    scale_count = clips_here * devices
    up_gradient = (
        lax.psum_scatter(
            row_contract(
                own_columns(normed, jnp.int32(0), up_weight.shape[0] * lax.axis_size("enc")),
                pre_grad,
            ),
            "enc",
            scatter_dimension=0,
            tiled=True,
        )
        / scale_count
    )
    down_gradient = (
        lax.psum_scatter(
            row_contract(
                own_columns(
                    post_rounded, jnp.int32(0), down_weight.shape[1] * lax.axis_size("enc")
                ),
                act_rounded,
            ),
            "enc",
            scatter_dimension=0,
            tiled=True,
        )
        / scale_count
    ).T
    return (input_gradient, up_gradient, down_gradient)


def solution(mesh):
    return jax.shard_map(
        shards,
        mesh=mesh,
        in_specs=(
            P("enc", None, "llm"),
            P(None, "llm"),
            P("enc"),
            P("enc"),
            P("enc"),
            P("enc", None, None),
            P("enc", None, None),
            P(),
            P(),
            P("enc", "llm"),
            P("llm"),
            P("llm", "enc"),
            P(),
        ),
        out_specs=(P("enc", None, "llm"), P("enc", "llm"), P("llm", "enc")),
        check_vma=False,
    )
```

profile of v0, /device:TPU:0, one launch (start us, length us, event | category | flops | bytes accessed | tf_op | source)
XLA Modules:
  0.0 444.9 jit_solution(10234905339764300413)
XLA Ops:
  9.7 8.4 %all-to-all-start = ((bf16[32,1,16]{2,1,0:T(2,128)(2,1)}), bf16[32,1,16]{2,1,0:T(2,128)(2,1)S(1)}, u32[]{:S(2)}, u32[]{:S(2)}) async-start(bf16[32,1,16]{2,1,0:T(2,128)(2,1)} %copy.26), calls=%async_computation | async-start | bytes 32768 | tf_op jit(solution)/shard_map/all_to_all | solution.py:62
  18.2 6.5 %copy.28 = bf16[8,128,2048]{2,0,1:T(8,128)(2,1)} copy(bf16[8,128,2048]{2,1,0:T(8,128)(2,1)} %param.13) | data formatting | bytes 8388608 | tf_op args[0]
  24.7 5.8 %gather_fusion = bf16[16,32,2048]{2,0,1:T(8,128)(2,1)S(1)} fusion(bf16[8,128,2048]{2,0,1:T(8,128)(2,1)} %copy.28, s32[16]{0:T(128)S(1)} %fusion.41), kind=kCustom, calls=%fused_computation | custom fusion | bytes 4194496 | tf_op jit(solution)/shard_map/vmap()/gather | solution.py:103
  31.9 4.3 copy.29
  36.1 7.7 %all-to-all-start.1 = ((bf16[32,1,32,2048]{3,2,1,0:T(8,128)(2,1)}), bf16[32,1,32,2048]{3,2,1,0:T(8,128)(2,1)}, u32[]{:S(2)}, u32[]{:S(2)}) async-start(bf16[32,1,32,2048]{3,2,1,0:T(8,128)(2,1)} %copy.29), calls=%async_computation.1 | async-start | bytes 8388608 | tf_op jit(solution)/shard_map/all_to_all | solution.py:61
  46.7 1.9 fusion.13
  48.6 49.8 %all-to-all-done.1 = bf16[32,1,32,2048]{3,2,1,0:T(8,128)(2,1)} async-done(((bf16[32,1,32,2048]{3,2,1,0:T(8,128)(2,1)}), bf16[32,1,32,2048]{3,2,1,0:T(8,128)(2,1)}, u32[]{:S(2)}, u32[]{:S(2)}) %all-to-all-start.1) | async-done | bytes 4194336 | tf_op jit(solution)/shard_map/all_to_all | solution.py:61
  98.4 6.8 %fusion.5 = bf16[16,32,2048]{2,0,1:T(8,128)(2,1)S(1)} fusion(bf16[32,1,32,2048]{3,2,1,0:T(8,128)(2,1)} %all-to-all-done.1, bf16[32,1,16]{0,2,1:T(8,128)(2,1)S(1)} %copy.27), kind=kOutput, calls=%fused_computation.10 | convolution fusion | flops 68157440 | bytes 6292480 | tf_op jit(solution)/shard_map/npc,npfw->cfw/dot_general | solution.py:64
  105.2 8.2 %fusion = f32[16,32,1280]{2,1,0:T(8,128)} fusion(bf16[1280,2048]{1,0:T(8,128)(2,1)} %param.14, bf16[16,32,2048]{2,0,1:T(8,128)(2,1)S(1)} %fusion.5), kind=kOutput, calls=%fused_computation.1 | convolution fusion | flops 2684354560 | bytes 9961472 | tf_op jit(solution)/shard_map/dot_general | solution.py:43
  113.4 54.4 %all-reduce.4 = bf16[16,32,1280]{2,1,0:T(8,128)(2,1)} all-reduce(f32[16,32,1280]{2,1,0:T(8,128)} %fusion), channel_id=1, replica_groups=mesh['llm'=4,'enc'=32] {'llm'}, use_global_device_ids=true, to_apply=%region_3.4 | all-reduce | flops 655360 | bytes 3932160 | tf_op jit(solution)/shard_map/psum | solution.py:50
  167.9 2.1 multiply_reduce_fusion.4
  170.2 3.7 fusion.17
  173.9 6.1 %convolution_add_fusion = f32[512,1280]{1,0:T(8,128)} fusion(bf16[1280,1280]{1,0:T(8,128)(2,1)} %all-gather.5.cloned.1.call-done, f32[1280]{0:T(1024)S(1)} %copy-done.6, f32[512,1280]{1,0:T(8,128)} %fusion.13, f32[1280]{0:T(1024)S(1)} %copy-done.7, f32[1280]{0:T(1024)S(1)} %copy-done.3), kind=kOutput, calls=%fused_computation.9 | convolution fusion | flops 1680343040 | bytes 8535040 | tf_op jit(solution)/shard_map/dot_general | solution.py:129
  180.0 5.9 %fusion.8 = bf16[512,1280]{1,0:T(8,128)(2,1)S(1)} fusion(bf16[1280,1280]{0,1:T(8,128)(2,1)} %all-gather.3.cloned.1.call-done, f32[512,1280]{1,0:T(8,128)} %convolution_add_fusion, f32[512,1280]{1,0:T(8,128)} %fusion.17), kind=kOutput, calls=%fused_computation.11 | convolution fusion | flops 1684930560 | bytes 9830400 | tf_op jit(solution)/shard_map/dot_general | solution.py:132
  185.9 3.4 fusion.47
  189.4 6.4 %fusion.30 = f32[1280,1280]{1,0:T(8,128)} fusion(bf16[512,1280]{1,0:T(8,128)(2,1)S(1)} %fusion.8, f32[512,1280]{1,0:T(8,128)} %fusion.13, f32[1280]{0:T(1024)S(1)} %copy-done.7, f32[1280]{0:T(1024)S(1)} %copy-done.3), kind=kOutput, calls=%fused_computation.51 | convolution fusion | flops 1679687680 | bytes 10496000 | tf_op jit(solution)/shard_map/dot_general | solution.py:31
  196.2 7.6 %fusion.22 = f32[1280,1280]{1,0:T(8,128)} fusion(f32[512,1280]{1,0:T(8,128)} %convolution_add_fusion, f32[512,1280]{1,0:T(8,128)} %fusion.17), kind=kOutput, calls=%fused_computation.37 | convolution fusion | flops 1681653760 | bytes 11796480 | tf_op jit(solution)/shard_map/dot_general | solution.py:31
  203.9 53.1 %all-reduce.3.cloned.1.call-done = f32[512,1280]{1,0:T(8,128)} async-done(((f32[512,1280]{1,0:T(8,128)}), f32[512,1280]{1,0:T(8,128)}) %all-reduce.3.cloned.1.call-update) | async-done | bytes 2621456 | tf_op jit(solution)/shard_map/psum | solution.py:142
  257.0 2.6 fusion.46
  259.6 3.3 fusion.25
  262.9 84.2 %reduce-scatter.3.cloned.1.call-done = f32[40,1280]{1,0:T(8,128)} async-done(((f32[1280,1280]{1,0:T(8,128)}), f32[40,1280]{1,0:T(8,128)}) %reduce-scatter.3.cloned.1.call-update) | async-done | bytes 204816 | tf_op jit(solution)/shard_map/reduce_scatter | solution.py:148
  347.2 1.6 broadcast_multiply_fusion.1
  348.8 87.9 %reduce-scatter.5.cloned.1.call-done = f32[40,1280]{1,0:T(8,128)} async-done(((f32[1280,1280]{1,0:T(8,128)}), f32[40,1280]{1,0:T(8,128)}) %reduce-scatter.5.cloned.1.call-update) | async-done | bytes 204816 | tf_op jit(solution)/shard_map/reduce_scatter | solution.py:160
  436.7 1.6 multiply_bitcast_fusion
  (57 shorter events, 7.3 us)
Async XLA Ops:
  7.2 166.7 %all-gather.5.cloned.1.call-start = ((), (), s32[]{:S(2)}) async-start(), calls=%async_computation.5 | async-start | bytes 3379200 | tf_op jit(solution)/shard_map/all_gather | solution.py:126
  9.7 26.4 %all-to-all-start = ((bf16[32,1,16]{2,1,0:T(2,128)(2,1)}), bf16[32,1,16]{2,1,0:T(2,128)(2,1)S(1)}, u32[]{:S(2)}, u32[]{:S(2)}) async-start(bf16[32,1,16]{2,1,0:T(2,128)(2,1)} %copy.26), calls=%async_computation | async-start | bytes 32768 | tf_op jit(solution)/shard_map/all_to_all | solution.py:62
  18.2 6.5 %copy-start.8 = (s32[16]{0:T(128)S(1)}, s32[16]{0:T(128)}, u32[]{:S(2)}) copy-start(s32[16]{0:T(128)} %param.16) | copy-start | bytes 196
  24.7 5.8 %copy-start.4 = (s32[16]{0:T(128)S(1)}, s32[16]{0:T(128)}, u32[]{:S(2)}) copy-start(s32[16]{0:T(128)} %param.15) | copy-start | bytes 196
  36.1 8.7 %copy-start = (bf16[16,32,1280]{2,1,0:T(8,128)(2,1)S(1)}, bf16[16,32,1280]{2,1,0:T(8,128)(2,1)}, u32[]{:S(2)}) copy-start(bf16[16,32,1280]{2,1,0:T(8,128)(2,1)} %param.19) | copy-start | bytes 3932164
  36.1 62.3 %all-to-all-start.1 = ((bf16[32,1,32,2048]{3,2,1,0:T(8,128)(2,1)}), bf16[32,1,32,2048]{3,2,1,0:T(8,128)(2,1)}, u32[]{:S(2)}, u32[]{:S(2)}) async-start(bf16[32,1,32,2048]{3,2,1,0:T(8,128)(2,1)} %copy.29), calls=%async_computation.1 | async-start | bytes 8388608 | tf_op jit(solution)/shard_map/all_to_all | solution.py:61
  43.9 1.9 copy-start.1
  43.9 136.1 %all-gather.3.cloned.1.call-start = ((), (), s32[]{:S(2)}) async-start(), calls=%async_computation.4 | async-start | bytes 3379200 | tf_op jit(solution)/shard_map/all_gather | solution.py:127
  44.6 212.4 %all-reduce.3.cloned.1.call-start = ((), (), s32[]{:S(2)}) async-start(), calls=%async_computation.6 | async-start | bytes 5242880 | tf_op jit(solution)/shard_map/psum | solution.py:142
  113.4 54.4 %copy-start.2 = (f32[1280]{0:T(1024)S(1)}, f32[1280]{0:T(1024)}, u32[]{:S(2)}) copy-start(f32[1280]{0:T(1024)} %param.25) | copy-start | bytes 15364
  170.1 3.7 copy-start.3
  170.1 3.7 copy-start.6
  170.2 3.7 copy-start.7
  180.0 5.9 %copy-start.5 = (bf16[1280,1280]{1,0:T(8,128)(2,1)S(1)}, bf16[1280,1280]{1,0:T(8,128)(2,1)}, u32[]{:S(2)}) copy-start(bf16[1280,1280]{1,0:T(8,128)(2,1)} %all-gather.5.cloned.1.call-done) | copy-start | bytes 9830404
  189.4 157.8 %reduce-scatter.3.cloned.1.call-start = ((), (), s32[]{:S(2)}) async-start(), calls=%async_computation.7 | async-start | bytes 6758400 | tf_op jit(solution)/shard_map/reduce_scatter | solution.py:148
  195.9 240.8 %reduce-scatter.5.cloned.1.call-start = ((), (), s32[]{:S(2)}) async-start(), calls=%async_computation.8 | async-start | bytes 6758400 | tf_op jit(solution)/shard_map/reduce_scatter | solution.py:160
Sparse Core Ops, SparseCore 0:
  10.3 74.7 all-gather.4
  87.5 55.1 all-gather.2
  189.5 67.4 all-reduce.2
  260.6 86.5 reduce-scatter.2
  350.8 85.8 reduce-scatter.4
where the time goes:
time: 445 us
  waiting for transfers between devices  276 us (62%)
  blocking collectives  54.4 us (12%)
  matrix products  46.2 us (10%)
  other arithmetic  19.2 us (4%)
  local copies, waits for them, and re-layouts  17.8 us (4%)
  starting transfers between devices  16.8 us (4%)
  between operations  13.9 us (3%)
    reduce_scatter x1, waiting for transfers between devices, shards(): lax.psum_scatter(row_contract(own_columns(post_rounded, jnp.int32(0), dow...  87.9 us
    reduce_scatter x1, waiting for transfers between devices, shards(): lax.psum_scatter(row_contract(own_columns(normed, jnp.int32(0), up_weight...  84.2 us
    psum x1, blocking collectives, project_sum(): return lax.psum(project_terms(clip_blocks, projection), 'llm')  54.4 us
    psum x1, waiting for transfers between devices, shards(): normed_grad = lax.psum(normed_part, 'llm')  53.1 us
    all_to_all x1, waiting for transfers between devices, deliver(): lax.all_to_all(packed, 'enc', split_axis=0, concat_axis=0, tiled=True)  49.8 us
    dot_general x2, matrix products, row_contract(): lax.dot_general(left_rows, right_rows, (((0,), (0,)), ((), ())), preferre...  14.1 us
  transfers between devices with their start and end apart: 7, of which 4 were waited for; matrix products, arithmetic and copies ran while one was open for 16% of the time, Pallas kernels for 0%

commit v1 on v0

--- a/solution.py
+++ b/solution.py
@@ -5,6 +5,12 @@
 
 CPS = 2
 norm_epsilon = 1e-05
+
+
+def gather_and_add(x, name):
+    parts = lax.all_gather(x, name, axis=0, tiled=False)
+    total = parts.sum(axis=0)
+    return total
 
 
 def gelu_parts(pre_act):
@@ -47,7 +53,7 @@
 
 
 def project_sum(clip_blocks, projection):
-    return lax.psum(project_terms(clip_blocks, projection), "llm")
+    return gather_and_add(project_terms(clip_blocks, projection), "llm")
 
 
 def deliver(clip_blocks, routing, slot_marks):

time: 445 us -> 531 us (1.19)
  waiting for transfers between devices: 276 us -> 409 us
  blocking collectives: 54.4 us -> 0 us
  other arithmetic: 19.2 us -> 25.5 us
    all_gather x0 -> x1, waiting for transfers between devices: none -> 93.2 us  [gather_and_add(): parts = lax.all_gather(x, name, axis=0, tiled=False)]
    psum x1 -> x0, blocking collectives: 54.4 us -> none  [project_sum(): return lax.psum(project_terms(clip_blocks, projection), 'llm')]
    all_gather x1, waiting for transfers between devices: 0.01 us -> 36.2 us  [shards(): lax.all_gather(down_weight, 'enc', axis=1, tiled=True)]
    reduce_sum x0 -> x1, other arithmetic: none -> 6.3 us  [gather_and_add(): total = parts.sum(axis=0)]
  transfers between devices with their start and end apart: 7 -> 8, of which waited for: 4 -> 6; matrix products, arithmetic and copies ran while one was open for 16% -> 15% of each run, Pallas kernels for 0% -> 0%
where the time goes in v1:
time: 531 us; the launch traced here: 530 us
  waiting for transfers between devices  409 us (77%)
  matrix products  46.1 us (9%)
  other arithmetic  25.5 us (5%)
  local copies, waits for them, and re-layouts  18.2 us (3%)
  starting transfers between devices  16.9 us (3%)
  between operations  14.2 us (3%)
    all_gather x1, waiting for transfers between devices, gather_and_add(): parts = lax.all_gather(x, name, axis=0, tiled=False)  93.2 us
    reduce_scatter x1, waiting for transfers between devices, shards(): lax.psum_scatter(row_contract(own_columns(post_rounded, jnp.int32(0), dow...  88 us
    reduce_scatter x1, waiting for transfers between devices, shards(): lax.psum_scatter(row_contract(own_columns(normed, jnp.int32(0), up_weight...  84.2 us
    all_to_all x1, waiting for transfers between devices, deliver(): lax.all_to_all(packed, 'enc', split_axis=0, concat_axis=0, tiled=True)  54.3 us
    psum x1, waiting for transfers between devices, shards(): normed_grad = lax.psum(normed_part, 'llm')  52.1 us
    all_gather x1, waiting for transfers between devices, shards(): lax.all_gather(down_weight, 'enc', axis=1, tiled=True)  36.2 us
    dot_general x2, matrix products, row_contract(): lax.dot_general(left_rows, right_rows, (((0,), (0,)), ((), ())), preferre...  14 us
  transfers between devices with their start and end apart: 8, of which 6 were waited for; matrix products, arithmetic and copies ran while one was open for 15% of the time, Pallas kernels for 0%

profile of v1, /device:TPU:0, one launch (start us, length us, event | category | flops | bytes accessed | tf_op | source)
XLA Modules:
  0.0 530.4 jit_solution(16177098980703635062)
XLA Ops:
  9.7 8.4 %all-to-all-start = ((bf16[32,1,16]{2,1,0:T(2,128)(2,1)}), bf16[32,1,16]{2,1,0:T(2,128)(2,1)S(1)}, u32[]{:S(2)}, u32[]{:S(2)}) async-start(bf16[32,1,16]{2,1,0:T(2,128)(2,1)} %copy.26), calls=%async_computation | async-start | bytes 32768 | tf_op jit(solution)/shard_map/all_to_all | solution.py:68
  18.2 6.5 %copy.28 = bf16[8,128,2048]{2,0,1:T(8,128)(2,1)} copy(bf16[8,128,2048]{2,1,0:T(8,128)(2,1)} %param.13) | data formatting | bytes 8388608 | tf_op args[0]
  24.7 5.8 %gather_fusion = bf16[16,32,2048]{2,0,1:T(8,128)(2,1)S(1)} fusion(bf16[8,128,2048]{2,0,1:T(8,128)(2,1)} %copy.28, s32[16]{0:T(128)S(1)} %fusion.41), kind=kCustom, calls=%fused_computation | custom fusion | bytes 4194496 | tf_op jit(solution)/shard_map/vmap()/gather | solution.py:109
  31.8 4.4 copy.29
  36.2 7.6 %all-to-all-start.1 = ((bf16[32,1,32,2048]{3,2,1,0:T(8,128)(2,1)}), bf16[32,1,32,2048]{3,2,1,0:T(8,128)(2,1)}, u32[]{:S(2)}, u32[]{:S(2)}) async-start(bf16[32,1,32,2048]{3,2,1,0:T(8,128)(2,1)} %copy.29), calls=%async_computation.1 | async-start | bytes 8388608 | tf_op jit(solution)/shard_map/all_to_all | solution.py:67
  44.1 54.3 %all-to-all-done.1 = bf16[32,1,32,2048]{3,2,1,0:T(8,128)(2,1)} async-done(((bf16[32,1,32,2048]{3,2,1,0:T(8,128)(2,1)}), bf16[32,1,32,2048]{3,2,1,0:T(8,128)(2,1)}, u32[]{:S(2)}, u32[]{:S(2)}) %all-to-all-start.1) | async-done | bytes 4194336 | tf_op jit(solution)/shard_map/all_to_all | solution.py:67
  98.4 6.8 %fusion.5 = bf16[16,32,2048]{2,0,1:T(8,128)(2,1)S(1)} fusion(bf16[32,1,32,2048]{3,2,1,0:T(8,128)(2,1)} %all-to-all-done.1, bf16[32,1,16]{0,2,1:T(8,128)(2,1)S(1)} %copy.27), kind=kOutput, calls=%fused_computation.10 | convolution fusion | flops 68157440 | bytes 6292480 | tf_op jit(solution)/shard_map/npc,npfw->cfw/dot_general | solution.py:70
  105.2 8.2 %fusion = f32[16,32,1280]{2,1,0:T(8,128)} fusion(bf16[1280,2048]{1,0:T(8,128)(2,1)} %param.14, bf16[16,32,2048]{2,0,1:T(8,128)(2,1)S(1)} %fusion.5), kind=kOutput, calls=%fused_computation.1 | convolution fusion | flops 2684354560 | bytes 9961472 | tf_op jit(solution)/shard_map/dot_general | solution.py:49
  116.6 1.9 fusion.13
  118.5 6.2 %convolution_add_fusion = f32[512,1280]{1,0:T(8,128)} fusion(bf16[1280,1280]{1,0:T(8,128)(2,1)} %all-gather.7.cloned.1.call-done, f32[1280]{0:T(1024)S(1)} %copy-done.6, f32[512,1280]{1,0:T(8,128)} %fusion.13, f32[1280]{0:T(1024)S(1)} %copy-done.7, f32[1280]{0:T(1024)S(1)} %copy-done.3), kind=kOutput, calls=%fused_computation.9 | convolution fusion | flops 1680343040 | bytes 8535040 | tf_op jit(solution)/shard_map/dot_general | solution.py:135
  124.6 93.2 %all-gather.9.cloned.1.call-done = f32[64,32,1280]{2,1,0:T(8,128)} async-done(((f32[16,32,1280]{2,1,0:T(8,128)}), f32[64,32,1280]{2,1,0:T(8,128)}) %all-gather.9.cloned.1.call-update) | async-done | bytes 10485776 | tf_op jit(solution)/shard_map/all_gather | solution.py:11
  217.8 6.3 %reduce_sum.93 = bf16[16,32,1280]{2,1,0:T(8,128)(2,1)} reduce(f32[4,16,32,1280]{3,2,1,0:T(8,128)} %bitcast.56, f32[]{:T(128)} %constant.66.clone.1), dimensions={0}, to_apply=%region_3.4 | reduce | flops 1966080 | bytes 11796484 | tf_op jit(solution)/shard_map/reduce_sum | solution.py:12
  224.1 2.1 multiply_reduce_fusion.4
  226.4 3.7 fusion.17
  230.1 36.2 %all-gather.5.cloned.1.call-done = bf16[1280,1280]{0,1:T(8,128)(2,1)} async-done(((bf16[1280,40]{0,1:T(8,128)(2,1)}), bf16[1280,1280]{0,1:T(8,128)(2,1)}) %all-gather.5.cloned.1.call-update) | async-done | bytes 3276816 | tf_op jit(solution)/shard_map/all_gather | solution.py:133
  266.3 5.9 %fusion.8 = bf16[512,1280]{1,0:T(8,128)(2,1)S(1)} fusion(bf16[1280,1280]{0,1:T(8,128)(2,1)} %all-gather.5.cloned.1.call-done, f32[512,1280]{1,0:T(8,128)} %convolution_add_fusion, f32[512,1280]{1,0:T(8,128)} %fusion.17), kind=kOutput, calls=%fused_computation.11 | convolution fusion | flops 1684930560 | bytes 9830400 | tf_op jit(solution)/shard_map/dot_general | solution.py:138
  272.2 3.4 fusion.47
  275.7 6.4 %fusion.30 = f32[1280,1280]{1,0:T(8,128)} fusion(bf16[512,1280]{1,0:T(8,128)(2,1)S(1)} %fusion.8, f32[512,1280]{1,0:T(8,128)} %fusion.13, f32[1280]{0:T(1024)S(1)} %copy-done.7, f32[1280]{0:T(1024)S(1)} %copy-done.3), kind=kOutput, calls=%fused_computation.51 | convolution fusion | flops 1679687680 | bytes 10496000 | tf_op jit(solution)/shard_map/dot_general | solution.py:37
  282.4 7.6 %fusion.22 = f32[1280,1280]{1,0:T(8,128)} fusion(f32[512,1280]{1,0:T(8,128)} %convolution_add_fusion, f32[512,1280]{1,0:T(8,128)} %fusion.17), kind=kOutput, calls=%fused_computation.37 | convolution fusion | flops 1681653760 | bytes 11796480 | tf_op jit(solution)/shard_map/dot_general | solution.py:37
  290.1 52.1 %all-reduce.2.cloned.1.call-done = f32[512,1280]{1,0:T(8,128)} async-done(((f32[512,1280]{1,0:T(8,128)}), f32[512,1280]{1,0:T(8,128)}) %all-reduce.2.cloned.1.call-update) | async-done | bytes 2621456 | tf_op jit(solution)/shard_map/psum | solution.py:148
  342.2 2.6 fusion.46
  344.8 3.3 fusion.25
  348.1 84.2 %reduce-scatter.3.cloned.1.call-done = f32[40,1280]{1,0:T(8,128)} async-done(((f32[1280,1280]{1,0:T(8,128)}), f32[40,1280]{1,0:T(8,128)}) %reduce-scatter.3.cloned.1.call-update) | async-done | bytes 204816 | tf_op jit(solution)/shard_map/reduce_scatter | solution.py:154
  434.0 88.0 %reduce-scatter.5.cloned.1.call-done = f32[40,1280]{1,0:T(8,128)} async-done(((f32[1280,1280]{1,0:T(8,128)}), f32[40,1280]{1,0:T(8,128)}) %reduce-scatter.5.cloned.1.call-update) | async-done | bytes 204816 | tf_op jit(solution)/shard_map/reduce_scatter | solution.py:166
  (60 shorter events, 11.1 us)
Async XLA Ops:
  7.2 111.3 %all-gather.7.cloned.1.call-start = ((), (), s32[]{:S(2)}) async-start(), calls=%async_computation.5 | async-start | bytes 3379200 | tf_op jit(solution)/shard_map/all_gather | solution.py:132
  9.7 26.5 %all-to-all-start = ((bf16[32,1,16]{2,1,0:T(2,128)(2,1)}), bf16[32,1,16]{2,1,0:T(2,128)(2,1)S(1)}, u32[]{:S(2)}, u32[]{:S(2)}) async-start(bf16[32,1,16]{2,1,0:T(2,128)(2,1)} %copy.26), calls=%async_computation | async-start | bytes 32768 | tf_op jit(solution)/shard_map/all_to_all | solution.py:68
  18.2 6.5 %copy-start.8 = (s32[16]{0:T(128)S(1)}, s32[16]{0:T(128)}, u32[]{:S(2)}) copy-start(s32[16]{0:T(128)} %param.16) | copy-start | bytes 196
  24.7 5.8 %copy-start.4 = (s32[16]{0:T(128)S(1)}, s32[16]{0:T(128)}, u32[]{:S(2)}) copy-start(s32[16]{0:T(128)} %param.15) | copy-start | bytes 196
  36.2 62.2 %all-to-all-start.1 = ((bf16[32,1,32,2048]{3,2,1,0:T(8,128)(2,1)}), bf16[32,1,32,2048]{3,2,1,0:T(8,128)(2,1)}, u32[]{:S(2)}, u32[]{:S(2)}) async-start(bf16[32,1,32,2048]{3,2,1,0:T(8,128)(2,1)} %copy.29), calls=%async_computation.1 | async-start | bytes 8388608 | tf_op jit(solution)/shard_map/all_to_all | solution.py:67
  43.8 174.0 %all-gather.9.cloned.1.call-start = ((), (), s32[]{:S(2)}) async-start(), calls=%async_computation.9 | async-start | bytes 13107200 | tf_op jit(solution)/shard_map/all_gather | solution.py:11
  113.4 1.3 copy-start
  113.4 2.2 copy-start.1
  113.4 152.8 %all-gather.5.cloned.1.call-start = ((), (), s32[]{:S(2)}) async-start(), calls=%async_computation.4 | async-start | bytes 3379200 | tf_op jit(solution)/shard_map/all_gather | solution.py:133
  114.2 228.0 %all-reduce.2.cloned.1.call-start = ((), (), s32[]{:S(2)}) async-start(), calls=%async_computation.6 | async-start | bytes 5242880 | tf_op jit(solution)/shard_map/psum | solution.py:148
  116.0 2.5 copy-start.3
  116.0 2.5 copy-start.6
  116.0 2.5 copy-start.7
  217.8 6.3 %copy-start.2 = (f32[1280]{0:T(1024)S(1)}, f32[1280]{0:T(1024)}, u32[]{:S(2)}) copy-start(f32[1280]{0:T(1024)} %param.25) | copy-start | bytes 15364
  266.3 5.9 %copy-start.5 = (bf16[1280,1280]{1,0:T(8,128)(2,1)S(1)}, bf16[1280,1280]{1,0:T(8,128)(2,1)}, u32[]{:S(2)}) copy-start(bf16[1280,1280]{1,0:T(8,128)(2,1)} %all-gather.7.cloned.1.call-done) | copy-start | bytes 9830404
  275.7 156.7 %reduce-scatter.3.cloned.1.call-start = ((), (), s32[]{:S(2)}) async-start(), calls=%async_computation.7 | async-start | bytes 6758400 | tf_op jit(solution)/shard_map/reduce_scatter | solution.py:154
  282.1 239.8 %reduce-scatter.5.cloned.1.call-start = ((), (), s32[]{:S(2)}) async-start(), calls=%async_computation.8 | async-start | bytes 6758400 | tf_op jit(solution)/shard_map/reduce_scatter | solution.py:166
Sparse Core Ops, SparseCore 0:
  10.3 74.9 all-gather.6
  113.6 104.1 all-gather.8
  220.1 46.1 all-gather.4
  275.8 66.3 all-reduce.1
  345.8 86.5 reduce-scatter.2
  436.0 85.9 reduce-scatter.4
